TPU v7x, 32 devices: a whole 2x2x4 slice. The times are simulated.
32 devices in a mesh: space: 16 (over z, x, core), tm: 2 (over y).
Axes of the slice: x: 2, y: 2, z: 4, core: 2. Of those that a mesh axis runs over, the one named last changes fastest.
Arguments:
- node_feats: bfloat16 [128, 7168, 128], P('tm', 'space'), may hold values from -6 to 6
- positions: float32 [128, 3, 7168], P('tm', None, 'space'), may hold values from -3 to 3
- neighbours: int32 [128, 224, 8], P('tm', 'space'), may hold values from 0 to 223, as said below
- edge_in: bfloat16 [256, 128], replicated, may hold values from -0.375 to 0.375
- edge_out: bfloat16 [128, 128], replicated, may hold values from -0.5 to 0.5
- edge_params: float32 [3, 128], replicated, may hold values from -3 to 3
- coord_weight: float32 [128], replicated, may hold values from -0.5 to 0.5
- spectral: bfloat16 [2, 64, 128, 128], replicated, may hold values from -0.375 to 0.375
- node_in: bfloat16 [256, 128], replicated, may hold values from -0.375 to 0.375
- node_out: bfloat16 [128, 128], replicated, may hold values from -0.5 to 0.5
- node_bias: float32 [2, 128], replicated, may hold values from -3 to 3
Outputs:
- new_feats: bfloat16 [128, 7168, 128], P('tm', 'space')
- new_positions: float32 [128, 3, 7168], P('tm', None, 'space')
Inputs may be any that keep to these rules, and one draw needn't show every extreme that they name: neighbours[f, b, s] = (b + o) mod 224 for an offset o with -6 <= o <= 6; the offsets of a block's list may repeat, and every list holds the offsets 0, -6 and +6 in some slots.
All inputs are finite; a program needn't handle non-finite values.
Results may differ from a plain program's by a relative error of at most 0.0065.
Values may be sent and summed in bfloat16 or wider, within the bound.
No kernel may reach another device: no remote copies, remote signals or barrier semaphores. Data moves between devices by JAX's collectives and lax.ppermute only.
A program may use at most 320 MiB of HBM per device.

v0:
```python
import math
import jax
import jax.numpy as jnp
from jax import lax
from jax.sharding import PartitionSpec as P

BLOCK = 32
GHOST = 6


def with_halo(block, sides, width):
    for axis, dim in sides:
        count = lax.axis_size(axis)
        forward = [(i, i + 1) for i in range(count - 1)]
        forward.append((count - 1, 0))
        backward = [(target, source) for source, target in forward]
        low = lax.ppermute(
            lax.slice_in_dim(block, block.shape[dim] - width, None, axis=dim), axis, forward
        )
        high = lax.ppermute(lax.slice_in_dim(block, 0, width, axis=dim), axis, backward)
        block = jnp.concatenate([low, block, high], axis=dim)
    return block


def split_parts(values):
    high_part = values.astype(jnp.bfloat16)
    low_part = (values - high_part.astype(jnp.float32)).astype(jnp.bfloat16)
    return (high_part, low_part)


def edge_pass(own_src, other_dst, own_pos, other_pos, picked, edge_out, edge_params, coord_weight):
    frames, own_blocks, block_len, feat_width = own_src.shape
    other_blocks = other_dst.shape[1]
    flat_dst = other_dst.reshape(frames, other_blocks, block_len * feat_width)
    dst_high, dst_low = split_parts(flat_dst)
    block_ids = jnp.arange(other_blocks, dtype=jnp.int32)
    summed = jnp.zeros(own_src.shape, jnp.float32)
    moved = jnp.zeros(own_pos.shape, jnp.float32)
    for slot_num in range(picked.shape[2]):
        chosen = picked[:, :, slot_num]
        select_f32 = (chosen[:, :, None] == block_ids[None, None, :]).astype(jnp.float32)
        select_bf = select_f32.astype(jnp.bfloat16)
        near_dst = jnp.einsum(
            "fbc,fcx->fbx", select_bf, dst_high, preferred_element_type=jnp.float32
        ) + jnp.einsum("fbc,fcx->fbx", select_bf, dst_low, preferred_element_type=jnp.float32)
        near_dst = near_dst.reshape(own_src.shape)
        near_pos = jnp.einsum(
            "fbc,fdcl->fdbl", select_f32, other_pos, precision=lax.Precision.HIGHEST
        )
        offset_vec = own_pos - near_pos
        dist_sq = jnp.sum(offset_vec * offset_vec, axis=1)
        pre_act = own_src + near_dst + edge_params[0] + dist_sq[..., None] * edge_params[1]
        hidden = jax.nn.silu(pre_act).astype(jnp.bfloat16)
        out_act = (
            jnp.dot(
                hidden.reshape(-1, feat_width), edge_out, preferred_element_type=jnp.float32
            ).reshape(pre_act.shape)
            + edge_params[2]
        )
        message = jax.nn.silu(out_act)
        summed = summed + message
        weight = jnp.sum(message * coord_weight, axis=-1) / (1.0 + jnp.sqrt(dist_sq + 1.0))
        moved = moved + offset_vec * weight[:, None]
    return (summed, moved)


def spectral_conv(msg_block, spectral, out_count):
    frame_count, item_count, feat_width = msg_block.shape
    mode_count = spectral.shape[1]
    mode_ids = jnp.arange(mode_count, dtype=jnp.int32)
    time_ids = jnp.arange(frame_count, dtype=jnp.int32)
    step_angle = 2.0 * math.pi / frame_count
    angles = (mode_ids[:, None] * time_ids[None, :] % frame_count).astype(jnp.float32) * step_angle
    forward = jnp.concatenate([jnp.cos(angles), -jnp.sin(angles)], axis=0)
    fwd_high, fwd_low = split_parts(forward)
    flat_msg = msg_block.reshape(frame_count, -1)
    coeffs = jnp.dot(fwd_high, flat_msg, preferred_element_type=jnp.float32) + jnp.dot(
        fwd_low, flat_msg, preferred_element_type=jnp.float32
    )
    coeffs = coeffs.astype(jnp.bfloat16).reshape(2, mode_count, item_count, feat_width)
    mixed_real = jnp.einsum(
        "knh,khg->kng", coeffs[0], spectral[0], preferred_element_type=jnp.float32
    ) - jnp.einsum("knh,khg->kng", coeffs[1], spectral[1], preferred_element_type=jnp.float32)
    mixed_imag = jnp.einsum(
        "knh,khg->kng", coeffs[0], spectral[1], preferred_element_type=jnp.float32
    ) + jnp.einsum("knh,khg->kng", coeffs[1], spectral[0], preferred_element_type=jnp.float32)
    out_times = jnp.arange(out_count, dtype=jnp.int32)
    back_angles = (out_times[:, None] * mode_ids[None, :] % frame_count).astype(
        jnp.float32
    ) * step_angle
    weights = (jnp.where(mode_ids == 0, 1.0, 2.0) / frame_count).astype(jnp.float32)
    inverse = jnp.concatenate(
        [jnp.cos(back_angles) * weights, -jnp.sin(back_angles) * weights], axis=1
    )
    inv_high, inv_low = split_parts(inverse)
    mixed_all = jnp.concatenate([mixed_real, mixed_imag], axis=0).reshape(2 * mode_count, -1)
    mix_high, mix_low = split_parts(mixed_all)
    conv_out = (
        jnp.dot(inv_high, mix_high, preferred_element_type=jnp.float32)
        + jnp.dot(inv_low, mix_high, preferred_element_type=jnp.float32)
        + jnp.dot(inv_high, mix_low, preferred_element_type=jnp.float32)
    )
    return conv_out.astype(jnp.bfloat16).reshape(out_count, item_count, feat_width)


def shards(
    node_feats,
    positions,
    neighbours,
    edge_in,
    edge_out,
    edge_params,
    coord_weight,
    spectral,
    node_in,
    node_out,
    node_bias,
):
    frames, local_rows, feat_width = node_feats.shape
    blocks = local_rows // BLOCK
    rim_rows = GHOST * BLOCK
    slot_count = neighbours.shape[2]
    slab_index = lax.axis_index("space")
    total_blocks = blocks * lax.axis_size("space")
    first_block = slab_index * blocks - GHOST
    ext_feats = with_halo(node_feats, (("space", 1),), rim_rows)
    ext_pos = with_halo(positions.astype(jnp.bfloat16), (("space", 2),), rim_rows).astype(
        positions.dtype
    )
    ext_pos4 = ext_pos.reshape(frames, 3, blocks + 2 * GHOST, BLOCK)
    own_src = jnp.dot(node_feats, edge_in[:feat_width], preferred_element_type=jnp.float32).reshape(
        frames, blocks, BLOCK, feat_width
    )
    own_pos = positions.reshape(frames, 3, blocks, BLOCK)
    picked = (neighbours - first_block) % total_blocks
    ext_dst = jnp.dot(ext_feats, edge_in[feat_width:], preferred_element_type=jnp.float32).reshape(
        frames, blocks + 2 * GHOST, BLOCK, feat_width
    )
    summed, moved = edge_pass(
        own_src, ext_dst, own_pos, ext_pos4, picked, edge_out, edge_params, coord_weight
    )
    mean_msg = (summed / slot_count).astype(jnp.bfloat16).reshape(frames, local_rows, feat_width)
    new_positions = positions + (moved / slot_count).reshape(frames, 3, local_rows)
    regrouped = lax.all_to_all(mean_msg, "tm", split_axis=1, concat_axis=0, tiled=True)
    conv_all = spectral_conv(regrouped, spectral, regrouped.shape[0])
    conv_own = lax.all_to_all(conv_all, "tm", split_axis=0, concat_axis=1, tiled=True)
    node_pre = (
        jnp.dot(node_feats, node_in[:feat_width], preferred_element_type=jnp.float32)
        + jnp.dot(conv_own, node_in[feat_width:], preferred_element_type=jnp.float32)
        + node_bias[0]
    )
    node_hidden = jax.nn.silu(node_pre).astype(jnp.bfloat16)
    new_feats = (
        node_feats.astype(jnp.float32)
        + (jnp.dot(node_hidden, node_out, preferred_element_type=jnp.float32) + node_bias[1])
    ).astype(jnp.bfloat16)
    return (new_feats, new_positions)


def solution(mesh):
    placed = (
        P("tm", "space", None),
        P("tm", None, "space"),
        P("tm", "space", None),
        P(),
        P(),
        P(),
        P(),
        P(),
        P(),
        P(),
        P(),
    )
    return jax.shard_map(
        shards,
        mesh=mesh,
        in_specs=placed,
        out_specs=(P("tm", "space", None), P("tm", None, "space")),
        check_vma=False,
    )
```

profile of v0, /device:TPU:1, one launch (start us, length us, event | category | flops | bytes accessed | tf_op | source)
XLA Modules:
  0.0 959.1 jit_solution(7866914278327090848)
XLA Ops:
  14.3 10.3 %fusion.99 = f32[64,448,128]{2,1,0:T(8,128)} fusion(bf16[64,448,128]{2,1,0:T(8,128)(2,1)} %param.11, bf16[256,128]{1,0:T(8,128)(2,1)S(1)} %copy-done.48), kind=kOutput, calls=%fused_computation.187 | convolution fusion | flops 939524096 | bytes 22052864 | tf_op jit(solution)/shard_map/dot_general | solution.py:131
  26.8 53.9 %collective-permute-done.2 = bf16[64,3,192]{0,2,1:T(8,128)(2,1)S(1)} collective-permute-done((bf16[64,3,192]{0,2,1:T(8,128)(2,1)}, bf16[64,3,192]{0,2,1:T(8,128)(2,1)S(1)}, u32[]{:S(2)}, u32[]{:S(2)}) %collective-permute-start.2) | collective-permute-done | bytes 73760 | tf_op jit(solution)/shard_map/ppermute | solution.py:17
  106.3 13.9 %fusion.3 = f32[64,832,128]{2,1,0:T(8,128)} fusion(bf16[64,192,128]{2,1,0:T(8,128)(2,1)} %collective-permute-done.1, bf16[64,448,128]{2,1,0:T(8,128)(2,1)} %param.11, bf16[64,192,128]{2,1,0:T(8,128)(2,1)} %collective-permute-done, bf16[256,128]{1,0:T(8,128)(2,1)S(1)} %copy-done.48), kind=kOutput, calls=%fused_computation.37 | convolution fusion | flops 1785724928 | bytes 40927232 | tf_op jit(solution)/shard_map/dot_general | solution.py:136
  120.1 28.5 %reshape_reshape.3 = f32[64,26,4096]{2,1,0:T(8,128)} reshape(f32[64,832,128]{2,1,0:T(8,128)} %fusion.3) | data formatting | bytes 54525952 | tf_op jit(solution)/shard_map/reshape;reshape | solution.py:34
  148.6 29.6 %subtract_convert_fusion = (bf16[64,26,4096]{2,1,0:T(8,128)(2,1)}, bf16[64,26,4096]{2,1,0:T(8,128)(2,1)S(1)}) fusion(f32[64,26,4096]{2,1,0:T(8,128)} %reshape_reshape.3), kind=kLoop, calls=%fused_computation.5 | loop fusion | flops 27262976 | bytes 54525952 | tf_op jit(solution)/shard_map/convert_element_type | solution.py:27
  178.2 7.1 fusion.52
  192.3 7.1 fusion.50
  199.4 7.4 fusion.49
  206.8 7.2 fusion.48
  221.0 7.1 fusion.46
  228.2 7.1 fusion.45
  235.3 18.9 %convolution_add_fusion.3 = f32[64,14,4096]{2,1,0:T(8,128)} fusion(f32[64,14,4096]{2,1,0:T(8,128)} %fusion.52, bf16[64,26,4096]{2,1,0:T(8,128)(2,1)} %get-tuple-element.18, s32[64,14]{1,0:T(8,128)S(1)} %copy.208), kind=kOutput, calls=%fused_computation.46 | convolution fusion | flops 194580736 | bytes 42995200 | tf_op jit(solution)/shard_map/fbc,fcx->fbx/dot_general | solution.py:45
  254.2 17.9 %reshape.371 = f32[64,14,32,128]{3,2,1,0:T(8,128)} reshape(f32[64,14,4096]{2,1,0:T(8,128)} %convolution_add_fusion.3) | data formatting | bytes 29360128 | tf_op jit(solution)/shard_map/reshape | solution.py:46
  272.1 18.9 %convolution_add_fusion.4 = f32[64,14,4096]{2,1,0:T(8,128)} fusion(f32[64,14,4096]{2,1,0:T(8,128)} %fusion.51, bf16[64,26,4096]{2,1,0:T(8,128)(2,1)} %get-tuple-element.18, s32[64,14]{1,0:T(8,128)S(1)} %copy.203), kind=kOutput, calls=%fused_computation.47 | convolution fusion | flops 194580736 | bytes 42995200 | tf_op jit(solution)/shard_map/fbc,fcx->fbx/dot_general | solution.py:45
  290.9 17.5 %reshape.370 = f32[64,14,32,128]{3,2,1,0:T(8,128)} reshape(f32[64,14,4096]{2,1,0:T(8,128)} %convolution_add_fusion.4) | data formatting | bytes 29360128 | tf_op jit(solution)/shard_map/reshape | solution.py:46
  308.4 18.9 %convolution_add_fusion.5 = f32[64,14,4096]{2,1,0:T(8,128)} fusion(f32[64,14,4096]{2,1,0:T(8,128)} %fusion.50, bf16[64,26,4096]{2,1,0:T(8,128)(2,1)} %get-tuple-element.18, s32[64,14]{1,0:T(8,128)S(1)} %copy.198), kind=kOutput, calls=%fused_computation.48 | convolution fusion | flops 194580736 | bytes 42995200 | tf_op jit(solution)/shard_map/fbc,fcx->fbx/dot_general | solution.py:45
  327.3 17.5 %reshape.369 = f32[64,14,32,128]{3,2,1,0:T(8,128)} reshape(f32[64,14,4096]{2,1,0:T(8,128)} %convolution_add_fusion.5) | data formatting | bytes 29360128 | tf_op jit(solution)/shard_map/reshape | solution.py:46
  344.8 19.0 %convolution_add_fusion.6 = f32[64,14,4096]{2,1,0:T(8,128)} fusion(f32[64,14,4096]{2,1,0:T(8,128)} %fusion.49, bf16[64,26,4096]{2,1,0:T(8,128)(2,1)} %get-tuple-element.18, s32[64,14]{1,0:T(8,128)S(1)} %copy-done.40), kind=kOutput, calls=%fused_computation.49 | convolution fusion | flops 194580736 | bytes 42995200 | tf_op jit(solution)/shard_map/fbc,fcx->fbx/dot_general | solution.py:45
  363.8 17.6 %reshape.368 = f32[64,14,32,128]{3,2,1,0:T(8,128)} reshape(f32[64,14,4096]{2,1,0:T(8,128)} %convolution_add_fusion.6) | data formatting | bytes 29360128 | tf_op jit(solution)/shard_map/reshape | solution.py:46
  381.4 19.0 %convolution_add_fusion.7 = f32[64,14,4096]{2,1,0:T(8,128)} fusion(f32[64,14,4096]{2,1,0:T(8,128)} %fusion.48, bf16[64,26,4096]{2,1,0:T(8,128)(2,1)} %get-tuple-element.18, s32[64,14]{1,0:T(8,128)S(1)} %copy-done.38), kind=kOutput, calls=%fused_computation.50 | convolution fusion | flops 194580736 | bytes 42995200 | tf_op jit(solution)/shard_map/fbc,fcx->fbx/dot_general | solution.py:45
  400.4 17.5 %reshape.367 = f32[64,14,32,128]{3,2,1,0:T(8,128)} reshape(f32[64,14,4096]{2,1,0:T(8,128)} %convolution_add_fusion.7) | data formatting | bytes 29360128 | tf_op jit(solution)/shard_map/reshape | solution.py:46
  417.9 18.9 %convolution_add_fusion.8 = f32[64,14,4096]{2,1,0:T(8,128)} fusion(f32[64,14,4096]{2,1,0:T(8,128)} %fusion.47, bf16[64,26,4096]{2,1,0:T(8,128)(2,1)} %get-tuple-element.18, s32[64,14]{1,0:T(8,128)S(1)} %copy-done.36), kind=kOutput, calls=%fused_computation.51 | convolution fusion | flops 194580736 | bytes 42995200 | tf_op jit(solution)/shard_map/fbc,fcx->fbx/dot_general | solution.py:45
  436.7 17.5 %reshape.366 = f32[64,14,32,128]{3,2,1,0:T(8,128)} reshape(f32[64,14,4096]{2,1,0:T(8,128)} %convolution_add_fusion.8) | data formatting | bytes 29360128 | tf_op jit(solution)/shard_map/reshape | solution.py:46
  454.2 18.9 %convolution_add_fusion.9 = f32[64,14,4096]{2,1,0:T(8,128)} fusion(f32[64,14,4096]{2,1,0:T(8,128)} %fusion.46, bf16[64,26,4096]{2,1,0:T(8,128)(2,1)} %get-tuple-element.18, s32[64,14]{1,0:T(8,128)S(1)} %copy-done.34), kind=kOutput, calls=%fused_computation.52 | convolution fusion | flops 194580736 | bytes 42995200 | tf_op jit(solution)/shard_map/fbc,fcx->fbx/dot_general | solution.py:45
  473.1 17.7 %reshape.365 = f32[64,14,32,128]{3,2,1,0:T(8,128)} reshape(f32[64,14,4096]{2,1,0:T(8,128)} %convolution_add_fusion.9) | data formatting | bytes 29360128 | tf_op jit(solution)/shard_map/reshape | solution.py:46
  490.8 18.9 %convolution_add_fusion.10 = f32[64,14,4096]{2,1,0:T(8,128)} fusion(f32[64,14,4096]{2,1,0:T(8,128)} %fusion.45, bf16[64,26,4096]{2,1,0:T(8,128)(2,1)} %get-tuple-element.18, s32[64,14]{1,0:T(8,128)S(1)} %copy-done.32), kind=kOutput, calls=%fused_computation.53 | convolution fusion | flops 194580736 | bytes 42995200 | tf_op jit(solution)/shard_map/fbc,fcx->fbx/dot_general | solution.py:45
  509.7 17.6 %reshape.364 = f32[64,14,32,128]{3,2,1,0:T(8,128)} reshape(f32[64,14,4096]{2,1,0:T(8,128)} %convolution_add_fusion.10) | data formatting | bytes 29360128 | tf_op jit(solution)/shard_map/reshape | solution.py:46
  527.5 20.7 %divide_multiply_fusion = f32[64,14,32,128]{3,2,1,0:T(8,128)} fusion(f32[128]{0:T(128)S(1)} %copy-done.53, f32[64,14,32,128]{3,2,1,0:T(8,128)} %bitcast.227, f32[64,14,32,128]{3,2,1,0:T(8,128)} %reshape.371, f32[64,14,32]{2,1,0:T(8,128)S(1)} %copy-done.16, f32[128]{0:T(128)S(1)} %copy-done.54, f32[128]{0:T(128)S(1)} %copy-done.52, ...), kind=kOutput, calls=%fused_computation.21 | convolution fusion | flops 990904320 | bytes 44189184 | tf_op jit(solution)/shard_map/dot_general | solution.py:55
  548.2 16.6 %divide_multiply_fusion.1 = f32[64,14,32,128]{3,2,1,0:T(8,128)} fusion(f32[128]{0:T(128)S(1)} %copy-done.53, f32[64,14,32,128]{3,2,1,0:T(8,128)S(1)} %bitcast.231, f32[64,14,32,128]{3,2,1,0:T(8,128)} %reshape.370, f32[64,14,32]{2,1,0:T(8,128)S(1)} %copy-done.18, f32[128]{0:T(128)S(1)} %copy-done.54, f32[128]{0:T(128)S(1)} %copy-done.52, ...), kind=kOutput, calls=%fused_computation.23 | convolution fusion | flops 990904320 | bytes 44189184 | tf_op jit(solution)/shard_map/dot_general | solution.py:55
  564.9 10.9 %divide_multiply_fusion.2 = f32[64,14,32,128]{3,2,1,0:T(8,128)} fusion(f32[128]{0:T(128)S(1)} %copy-done.53, f32[64,14,32,128]{3,2,1,0:T(8,128)S(1)} %bitcast.232, f32[64,14,32,128]{3,2,1,0:T(8,128)S(1)} %bitcast.243, f32[64,14,32]{2,1,0:T(8,128)S(1)} %copy-done.20, f32[128]{0:T(128)S(1)} %copy-done.54, f32[128]{0:T(128)S(1)} %copy-done.52, ...), kind=kOutput, calls=%fused_computation.25 | convolution fusion | flops 990904320 | bytes 44189184 | tf_op jit(solution)/shard_map/dot_general | solution.py:55
  575.8 17.8 %divide_multiply_fusion.3 = f32[64,14,32,128]{3,2,1,0:T(8,128)} fusion(f32[128]{0:T(128)S(1)} %copy-done.53, f32[64,14,32,128]{3,2,1,0:T(8,128)S(1)} %bitcast.233, f32[64,14,32,128]{3,2,1,0:T(8,128)} %reshape.368, f32[64,14,32]{2,1,0:T(8,128)S(1)} %copy-done.22, f32[128]{0:T(128)S(1)} %copy-done.54, f32[128]{0:T(128)S(1)} %copy-done.52, ...), kind=kOutput, calls=%fused_computation.27 | convolution fusion | flops 990904320 | bytes 44189184 | tf_op jit(solution)/shard_map/dot_general | solution.py:55
  593.6 10.9 %divide_multiply_fusion.4 = f32[64,14,32,128]{3,2,1,0:T(8,128)} fusion(f32[128]{0:T(128)S(1)} %copy-done.53, f32[64,14,32,128]{3,2,1,0:T(8,128)S(1)} %bitcast.234, f32[64,14,32,128]{3,2,1,0:T(8,128)S(1)} %copy-done.4, f32[64,14,32]{2,1,0:T(8,128)S(1)} %copy-done.24, f32[128]{0:T(128)S(1)} %copy-done.54, f32[128]{0:T(128)S(1)} %copy-done.52, ...), kind=kOutput, calls=%fused_computation.29 | convolution fusion | flops 990904320 | bytes 44189184 | tf_op jit(solution)/shard_map/dot_general | solution.py:55
  604.5 17.8 %divide_multiply_fusion.5 = f32[64,14,32,128]{3,2,1,0:T(8,128)} fusion(f32[128]{0:T(128)S(1)} %copy-done.53, f32[64,14,32,128]{3,2,1,0:T(8,128)S(1)} %bitcast.235, f32[64,14,32,128]{3,2,1,0:T(8,128)} %reshape.366, f32[64,14,32]{2,1,0:T(8,128)S(1)} %copy-done.26, f32[128]{0:T(128)S(1)} %copy-done.54, f32[128]{0:T(128)S(1)} %copy-done.52, ...), kind=kOutput, calls=%fused_computation.31 | convolution fusion | flops 990904320 | bytes 44189184 | tf_op jit(solution)/shard_map/dot_general | solution.py:55
  622.4 10.9 %divide_multiply_fusion.6 = f32[64,14,32,128]{3,2,1,0:T(8,128)} fusion(f32[128]{0:T(128)S(1)} %copy-done.53, f32[64,14,32,128]{3,2,1,0:T(8,128)S(1)} %bitcast.236, f32[64,14,32,128]{3,2,1,0:T(8,128)S(1)} %copy-done.5, f32[64,14,32]{2,1,0:T(8,128)S(1)} %copy-done.28, f32[128]{0:T(128)S(1)} %copy-done.54, f32[128]{0:T(128)S(1)} %copy-done.52, ...), kind=kOutput, calls=%fused_computation.33 | convolution fusion | flops 990904320 | bytes 44189184 | tf_op jit(solution)/shard_map/dot_general | solution.py:55
  633.2 52.7 %multiply_reduce_fusion.7 = (f32[64,14,32]{2,1,0:T(8,128)}, f32[64,14,32]{2,1,0:T(8,128)}, f32[64,14,32]{2,1,0:T(8,128)}, f32[64,14,32]{2,1,0:T(8,128)}, f32[64,...) fusion(f32[128]{0:T(128)S(1)} %copy-done.56, ...), kind=kOutput, calls=%fused_computation.17 | convolution fusion | flops 1082425344 | bytes 140527616 | tf_op jit(solution)/shard_map/dot_general | solution.py:55
  685.9 10.8 %copy.213 = bf16[64,448,128]{2,0,1:T(8,128)(2,1)} copy(bf16[64,448,128]{2,1,0:T(8,128)(2,1)} %bitcast.245) | data formatting | bytes 14680064 | tf_op jit(solution)/shard_map/reshape | solution.py:142
  703.8 47.5 %all-to-all-done = bf16[64,448,128]{2,0,1:T(8,128)(2,1)} async-done(((bf16[64,448,128]{2,0,1:T(8,128)(2,1)}), bf16[64,448,128]{2,0,1:T(8,128)(2,1)}, u32[]{:S(2)}, u32[]{:S(2)}) %all-to-all-start) | async-done | bytes 7340064 | tf_op jit(solution)/shard_map/all_to_all | solution.py:144
  751.3 7.8 copy.215
  762.2 8.1 fusion.11
  770.3 13.5 %fusion = bf16[128,28672]{1,0:T(8,128)(2,1)} fusion(f32[128,28672]{1,0:T(8,128)} %fusion.11, bf16[16,8,224,128]{3,2,1,0:T(8,128)(2,1)} %bitcast.226, f32[64,128]{1,0:T(8,128)S(1)} %get-tuple-element.66, f32[64,128]{1,0:T(8,128)S(1)} %get-tuple-element.67), kind=kOutput, calls=%fused_computation.3 | convolution fusion | flops 946946048 | bytes 29425664 | tf_op jit(solution)/shard_map/dot_general | solution.py:77
  811.6 14.5 %fusion.15 = f32[128,28672]{1,0:T(8,128)} fusion(f32[16,8,224,128]{3,2,1,0:T(8,128)S(1)} %bitcast.222, f32[128,64]{0,1:T(8,128)S(1)} %get-tuple-element.41, f32[128,64]{0,1:T(8,128)S(1)} %get-tuple-element.40), kind=kOutput, calls=%fused_computation.56 | convolution fusion | flops 939589632 | bytes 29425664 | tf_op jit(solution)/shard_map/dot_general | solution.py:99
  826.1 24.5 %convolution_add_fusion.1 = f32[128,28672]{1,0:T(8,128)} fusion(f32[128,28672]{1,0:T(8,128)} %fusion.15, f32[16,8,224,128]{3,2,1,0:T(8,128)} %bitcast.223, f32[128,64]{0,1:T(8,128)S(1)} %get-tuple-element.41, f32[128,64]{0,1:T(8,128)S(1)} %get-tuple-element.40), kind=kOutput, calls=%fused_computation.1 | convolution fusion | flops 943276032 | bytes 44105728 | tf_op jit(solution)/shard_map/dot_general | solution.py:100
  850.6 22.7 %fusion.16 = bf16[16,8,224,128]{3,1,2,0:T(8,128)(2,1)} fusion(f32[128,28672]{1,0:T(8,128)} %convolution_add_fusion.1, f32[16,8,224,128]{3,2,1,0:T(8,128)} %bitcast.224, f32[128,64]{0,1:T(8,128)S(1)} %get-tuple-element.41, f32[128,64]{0,1:T(8,128)S(1)} %get-tuple-element.40), kind=kOutput, calls=%fused_computation.57 | convolution fusion | flops 961609728 | bytes 36765696 | tf_op jit(solution)/shard_map/dot_general | solution.py:101
  873.3 7.8 copy.242
  888.0 12.7 %fusion.101 = f32[64,448,128]{2,1,0:T(8,128)} fusion(bf16[64,448,128]{2,1,0:T(8,128)(2,1)} %param.11, bf16[256,128]{1,0:T(8,128)(2,1)S(1)} %copy-done.49), kind=kOutput, calls=%fused_computation.189 | convolution fusion | flops 939524096 | bytes 22052864 | tf_op jit(solution)/shard_map/dot_general | solution.py:148
  911.4 25.3 %all-to-all-done.1 = bf16[128,224,128]{2,1,0:T(8,128)(2,1)} async-done(((bf16[128,224,128]{2,1,0:T(8,128)(2,1)}), bf16[128,224,128]{2,1,0:T(8,128)(2,1)}, u32[]{:S(2)}, u32[]{:S(2)}) %all-to-all-start.1) | async-done | bytes 7340064 | tf_op jit(solution)/shard_map/all_to_all | solution.py:146
  936.7 7.2 copy.216
  943.9 14.9 %add_convert_fusion = bf16[64,448,128]{2,1,0:T(8,128)(2,1)} fusion(bf16[64,448,128]{2,1,0:T(8,128)(2,1)} %param.11, f32[128]{0:T(128)S(1)} %get-tuple-element.39, f32[64,448,128]{2,1,0:T(8,128)} %fusion.101, bf16[64,448,128]{2,1,0:T(8,128)(2,1)} %bitcast.246, f32[128]{0:T(128)S(1)} %get-tuple-element.38, bf16[128,128]{1,0:T(8,128)(2,1)S(1)} %copy-done.55, ...), kind=kOutput, calls=%fused_computation.18 | convolution fusion | flops 1919418368 | bytes 36766720 | tf_op jit(solution)/shard_map/dot_general | solution.py:155
  (189 shorter events, 110.7 us)
Async XLA Ops:
  0.6 526.7 %copy-start = (bf16[128,128]{1,0:T(8,128)(2,1)S(1)}, bf16[128,128]{1,0:T(8,128)(2,1)}, u32[]{:S(2)}) copy-start(bf16[128,128]{1,0:T(8,128)(2,1)} %param.15) | copy-start | bytes 98308
  6.7 99.5 %collective-permute-start = (bf16[64,192,128]{2,1,0:T(8,128)(2,1)}, bf16[64,192,128]{2,1,0:T(8,128)(2,1)}, u32[]{:S(2)}, u32[]{:S(2)}) collective-permute-start(bf16[64,192,128]{2,1,0:T(8,128)(2,1)} %get-tuple-element.23), channel_id=1, source_target_pairs={{0,2},{2,4},{4,6},{6,8},{8,10},{10,12},{12,14},{14,16},{16,18},{18... | collective-permute-start | bytes 9437192 | tf_op jit(solution)/shard_map/ppermute | solution.py:17
  9.3 96.9 %collective-permute-start.1 = (bf16[64,192,128]{2,1,0:T(8,128)(2,1)}, bf16[64,192,128]{2,1,0:T(8,128)(2,1)}, u32[]{:S(2)}, u32[]{:S(2)}) collective-permute-start(bf16[64,192,128]{2,1,0:T(8,128)(2,1)} %get-tuple-element.24), channel_id=1, source_target_pairs={{2,0},{4,2},{6,4},{8,6},{10,8},{12,10},{14,12},{16,14},{18,16},{20... | collective-permute-start | bytes 9437192 | tf_op jit(solution)/shard_map/ppermute | solution.py:20
  11.4 69.3 %collective-permute-start.2 = (bf16[64,3,192]{0,2,1:T(8,128)(2,1)}, bf16[64,3,192]{0,2,1:T(8,128)(2,1)S(1)}, u32[]{:S(2)}, u32[]{:S(2)}) collective-permute-start(bf16[64,3,192]{0,2,1:T(8,128)(2,1)} %get-tuple-element.25), channel_id=1, source_target_pairs={{0,2},{2,4},{4,6},{6,8},{8,10},{10,12},{12,14},{14,16},{16,18},{18... | collective-permute-start | bytes 221192 | tf_op jit(solution)/shard_map/ppermute | solution.py:17
  13.2 69.9 %collective-permute-start.3 = (bf16[64,3,192]{0,2,1:T(8,128)(2,1)S(1)}, bf16[64,3,192]{0,2,1:T(8,128)(2,1)S(1)}, u32[]{:S(2)}, u32[]{:S(2)}) collective-permute-start(bf16[64,3,192]{0,2,1:T(8,128)(2,1)S(1)} %get-tuple-element.26), channel_id=1, source_target_pairs={{2,0},{4,2},{6,4},{8,6},{10,8},{12,10},{14,12},{16,14},{18,16},{20... | collective-permute-start | bytes 221192 | tf_op jit(solution)/shard_map/ppermute | solution.py:20
  26.4 173.0 %copy-start.39 = (s32[64,14]{1,0:T(8,128)}, s32[64,14]{1,0:T(8,128)S(1)}, u32[]{:S(2)}) copy-start(s32[64,14]{1,0:T(8,128)S(1)} %copy.193) | copy-start | bytes 10756
  26.5 180.3 %copy-start.37 = (s32[64,14]{1,0:T(8,128)}, s32[64,14]{1,0:T(8,128)S(1)}, u32[]{:S(2)}) copy-start(s32[64,14]{1,0:T(8,128)S(1)} %copy.188) | copy-start | bytes 10756
  26.6 187.4 %copy-start.35 = (s32[64,14]{1,0:T(8,128)}, s32[64,14]{1,0:T(8,128)S(1)}, u32[]{:S(2)}) copy-start(s32[64,14]{1,0:T(8,128)S(1)} %copy.183) | copy-start | bytes 10756
  26.7 194.3 %copy-start.33 = (s32[64,14]{1,0:T(8,128)}, s32[64,14]{1,0:T(8,128)S(1)}, u32[]{:S(2)}) copy-start(s32[64,14]{1,0:T(8,128)S(1)} %copy.178) | copy-start | bytes 10756
  26.8 201.3 %copy-start.31 = (s32[64,14]{1,0:T(8,128)}, s32[64,14]{1,0:T(8,128)S(1)}, u32[]{:S(2)}) copy-start(s32[64,14]{1,0:T(8,128)S(1)} %copy.171) | copy-start | bytes 10756
  327.3 17.5 %copy-start.40 = (s32[64,14]{1,0:T(8,128)S(1)}, s32[64,14]{1,0:T(8,128)}, u32[]{:S(2)}) copy-start(s32[64,14]{1,0:T(8,128)} %copy-done.39) | copy-start | bytes 10756
  363.8 17.6 %copy-start.38 = (s32[64,14]{1,0:T(8,128)S(1)}, s32[64,14]{1,0:T(8,128)}, u32[]{:S(2)}) copy-start(s32[64,14]{1,0:T(8,128)} %copy-done.37) | copy-start | bytes 10756
  400.4 17.5 %copy-start.36 = (s32[64,14]{1,0:T(8,128)S(1)}, s32[64,14]{1,0:T(8,128)}, u32[]{:S(2)}) copy-start(s32[64,14]{1,0:T(8,128)} %copy-done.35) | copy-start | bytes 10756
  436.7 17.5 %copy-start.34 = (s32[64,14]{1,0:T(8,128)S(1)}, s32[64,14]{1,0:T(8,128)}, u32[]{:S(2)}) copy-start(s32[64,14]{1,0:T(8,128)} %copy-done.33) | copy-start | bytes 10756
  473.1 17.7 %copy-start.32 = (s32[64,14]{1,0:T(8,128)S(1)}, s32[64,14]{1,0:T(8,128)}, u32[]{:S(2)}) copy-start(s32[64,14]{1,0:T(8,128)} %copy-done.31) | copy-start | bytes 10756
  509.7 17.7 %copy-start.16 = (f32[64,14,32]{2,1,0:T(8,128)S(1)}, f32[64,14,32]{2,1,0:T(8,128)}, u32[]{:S(2)}) copy-start(f32[64,14,32]{2,1,0:T(8,128)} %get-tuple-element.56) | copy-start | bytes 344068
  509.7 17.7 %copy-start.52 = (f32[128]{0:T(128)S(1)}, f32[128]{0:T(128)}, u32[]{:S(2)}) copy-start(f32[128]{0:T(128)} %get-tuple-element.35) | copy-start | bytes 1540
  509.7 17.7 %copy-start.53 = (f32[128]{0:T(128)S(1)}, f32[128]{0:T(128)}, u32[]{:S(2)}) copy-start(f32[128]{0:T(128)} %get-tuple-element.36) | copy-start | bytes 1540
  509.7 17.7 %copy-start.54 = (f32[128]{0:T(128)S(1)}, f32[128]{0:T(128)}, u32[]{:S(2)}) copy-start(f32[128]{0:T(128)} %get-tuple-element.37) | copy-start | bytes 1540
  509.7 38.4 %slice-start = ((s8[14680064]{0:T(1024)(128)(4,1)}), s8[2097152]{0:T(1024)(128)(4,1)S(1)}, s32[]{:S(2)}) async-start(s8[14680064]{0:T(1024)(128)(4,1)} %bitcast.229), calls=%async_computation.2 | async-start | bytes 4194304
  527.4 20.8 %slice-start.1 = ((s8[14680064]{0:T(1024)(128)(4,1)}), s8[4194304]{0:T(1024)(128)(4,1)S(1)}, s32[]{:S(2)}) async-start(s8[14680064]{0:T(1024)(128)(4,1)} %bitcast.229), calls=%async_computation.3 | async-start | bytes 8388608
  527.4 20.8 %slice-start.2 = ((s8[14680064]{0:T(1024)(128)(4,1)}), s8[4194304]{0:T(1024)(128)(4,1)S(1)}, s32[]{:S(2)}) async-start(s8[14680064]{0:T(1024)(128)(4,1)} %bitcast.229), calls=%async_computation.4 | async-start | bytes 8388608
  527.4 20.8 %slice-start.3 = ((s8[14680064]{0:T(1024)(128)(4,1)}), s8[4194304]{0:T(1024)(128)(4,1)S(1)}, s32[]{:S(2)}) async-start(s8[14680064]{0:T(1024)(128)(4,1)} %bitcast.229), calls=%async_computation.5 | async-start | bytes 8388608
  527.4 20.8 %copy-start.18 = (f32[64,14,32]{2,1,0:T(8,128)S(1)}, f32[64,14,32]{2,1,0:T(8,128)}, u32[]{:S(2)}) copy-start(f32[64,14,32]{2,1,0:T(8,128)} %get-tuple-element.54) | copy-start | bytes 344068
  527.4 37.4 %slice-start.4 = ((s8[14680064]{0:T(1024)(128)(4,1)}), s8[4194304]{0:T(1024)(128)(4,1)S(1)}, s32[]{:S(2)}) async-start(s8[14680064]{0:T(1024)(128)(4,1)} %bitcast.242), calls=%async_computation.6 | async-start | bytes 8388608
  527.4 37.4 %slice-start.5 = ((s8[14680064]{0:T(1024)(128)(4,1)}), s8[4194304]{0:T(1024)(128)(4,1)S(1)}, s32[]{:S(2)}) async-start(s8[14680064]{0:T(1024)(128)(4,1)} %bitcast.242), calls=%async_computation.7 | async-start | bytes 8388608
  548.2 16.7 %slice-start.6 = ((s8[14680064]{0:T(1024)(128)(4,1)}), s8[4194304]{0:T(1024)(128)(4,1)S(1)}, s32[]{:S(2)}) async-start(s8[14680064]{0:T(1024)(128)(4,1)} %bitcast.242), calls=%async_computation.8 | async-start | bytes 8388608
  548.2 16.6 %slice-start.7 = ((s8[14680064]{0:T(1024)(128)(4,1)}), s8[2097152]{0:T(1024)(128)(4,1)S(1)}, s32[]{:S(2)}) async-start(s8[14680064]{0:T(1024)(128)(4,1)} %bitcast.242), calls=%async_computation.9 | async-start | bytes 4194304
  548.2 16.6 %copy-start.20 = (f32[64,14,32]{2,1,0:T(8,128)S(1)}, f32[64,14,32]{2,1,0:T(8,128)}, u32[]{:S(2)}) copy-start(f32[64,14,32]{2,1,0:T(8,128)} %get-tuple-element.52) | copy-start | bytes 344068
  575.8 17.9 %copy-start.4 = (f32[64,14,32,128]{3,2,1,0:T(8,128)S(1)}, f32[64,14,32,128]{3,2,1,0:T(8,128)}, u32[]{:S(2)}) copy-start(f32[64,14,32,128]{3,2,1,0:T(8,128)} %reshape.367) | copy-start | bytes 44040196
  575.8 17.9 %copy-start.24 = (f32[64,14,32]{2,1,0:T(8,128)S(1)}, f32[64,14,32]{2,1,0:T(8,128)}, u32[]{:S(2)}) copy-start(f32[64,14,32]{2,1,0:T(8,128)} %get-tuple-element.48) | copy-start | bytes 344068
  604.5 17.9 %copy-start.5 = (f32[64,14,32,128]{3,2,1,0:T(8,128)S(1)}, f32[64,14,32,128]{3,2,1,0:T(8,128)}, u32[]{:S(2)}) copy-start(f32[64,14,32,128]{3,2,1,0:T(8,128)} %reshape.365) | copy-start | bytes 44040196
  604.5 17.9 %copy-start.28 = (f32[64,14,32]{2,1,0:T(8,128)S(1)}, f32[64,14,32]{2,1,0:T(8,128)}, u32[]{:S(2)}) copy-start(f32[64,14,32]{2,1,0:T(8,128)} %get-tuple-element.44) | copy-start | bytes 344068
  696.8 54.5 %all-to-all-start = ((bf16[64,448,128]{2,0,1:T(8,128)(2,1)}), bf16[64,448,128]{2,0,1:T(8,128)(2,1)}, u32[]{:S(2)}, u32[]{:S(2)}) async-start(bf16[64,448,128]{2,0,1:T(8,128)(2,1)} %copy.213), calls=%async_computation | async-start | bytes 14680064 | tf_op jit(solution)/shard_map/all_to_all | solution.py:144
  881.1 55.6 %all-to-all-start.1 = ((bf16[128,224,128]{2,1,0:T(8,128)(2,1)}), bf16[128,224,128]{2,1,0:T(8,128)(2,1)}, u32[]{:S(2)}, u32[]{:S(2)}) async-start(bf16[128,224,128]{2,1,0:T(8,128)(2,1)} %bitcast.241), calls=%async_computation.1 | async-start | bytes 14680064 | tf_op jit(solution)/shard_map/all_to_all | solution.py:146
  887.8 15.5 %copy-start.21 = (f32[64,14,32]{2,1,0:T(8,128)S(1)}, f32[64,14,32]{2,1,0:T(8,128)}, u32[]{:S(2)}) copy-start(f32[64,14,32]{2,1,0:T(8,128)} %get-tuple-element.52) | copy-start | bytes 344068
  887.8 15.5 %copy-start.23 = (f32[64,14,32]{2,1,0:T(8,128)S(1)}, f32[64,14,32]{2,1,0:T(8,128)}, u32[]{:S(2)}) copy-start(f32[64,14,32]{2,1,0:T(8,128)} %get-tuple-element.50) | copy-start | bytes 344068
  887.9 16.8 %copy-start.17 = (f32[64,14,32]{2,1,0:T(8,128)S(1)}, f32[64,14,32]{2,1,0:T(8,128)}, u32[]{:S(2)}) copy-start(f32[64,14,32]{2,1,0:T(8,128)} %get-tuple-element.56) | copy-start | bytes 344068
  887.9 16.8 %copy-start.19 = (f32[64,14,32]{2,1,0:T(8,128)S(1)}, f32[64,14,32]{2,1,0:T(8,128)}, u32[]{:S(2)}) copy-start(f32[64,14,32]{2,1,0:T(8,128)} %get-tuple-element.54) | copy-start | bytes 344068
  887.9 18.2 %copy-start.8 = (f32[64,3,14,32]{3,2,1,0:T(8,128)S(1)}, f32[64,3,14,32]{3,2,1,0:T(8,128)}, u32[]{:S(2)}) copy-start(f32[64,3,14,32]{3,2,1,0:T(8,128)} %get-tuple-element.57) | copy-start | bytes 1032196
  887.9 18.2 %copy-start.9 = (f32[64,3,14,32]{3,2,1,0:T(8,128)S(1)}, f32[64,3,14,32]{3,2,1,0:T(8,128)}, u32[]{:S(2)}) copy-start(f32[64,3,14,32]{3,2,1,0:T(8,128)} %get-tuple-element.55) | copy-start | bytes 1032196
  887.9 18.1 %copy-start.10 = (f32[64,3,14,32]{3,2,1,0:T(8,128)S(1)}, f32[64,3,14,32]{3,2,1,0:T(8,128)}, u32[]{:S(2)}) copy-start(f32[64,3,14,32]{3,2,1,0:T(8,128)} %get-tuple-element.53) | copy-start | bytes 1032196
  887.9 18.1 %copy-start.11 = (f32[64,3,14,32]{3,2,1,0:T(8,128)S(1)}, f32[64,3,14,32]{3,2,1,0:T(8,128)}, u32[]{:S(2)}) copy-start(f32[64,3,14,32]{3,2,1,0:T(8,128)} %get-tuple-element.51) | copy-start | bytes 1032196
  887.9 18.1 %copy-start.12 = (f32[64,3,14,32]{3,2,1,0:T(8,128)S(1)}, f32[64,3,14,32]{3,2,1,0:T(8,128)}, u32[]{:S(2)}) copy-start(f32[64,3,14,32]{3,2,1,0:T(8,128)} %get-tuple-element.49) | copy-start | bytes 1032196
  887.9 18.1 %copy-start.13 = (f32[64,3,14,32]{3,2,1,0:T(8,128)S(1)}, f32[64,3,14,32]{3,2,1,0:T(8,128)}, u32[]{:S(2)}) copy-start(f32[64,3,14,32]{3,2,1,0:T(8,128)} %get-tuple-element.47) | copy-start | bytes 1032196
  887.9 18.1 %copy-start.14 = (f32[64,3,14,32]{3,2,1,0:T(8,128)S(1)}, f32[64,3,14,32]{3,2,1,0:T(8,128)}, u32[]{:S(2)}) copy-start(f32[64,3,14,32]{3,2,1,0:T(8,128)} %get-tuple-element.45) | copy-start | bytes 1032196
  888.0 18.1 %copy-start.15 = (f32[64,3,14,32]{3,2,1,0:T(8,128)S(1)}, f32[64,3,14,32]{3,2,1,0:T(8,128)}, u32[]{:S(2)}) copy-start(f32[64,3,14,32]{3,2,1,0:T(8,128)} %get-tuple-element.43) | copy-start | bytes 1032196
  906.1 37.7 %copy-start.55 = (bf16[128,128]{1,0:T(8,128)(2,1)S(1)}, bf16[128,128]{1,0:T(8,128)(2,1)}, u32[]{:S(2)}) copy-start(bf16[128,128]{1,0:T(8,128)(2,1)} %param.20) | copy-start | bytes 98308
  (23 other events, 269.1 us)
where the time goes:
time: 967 us; the launch traced here: 959 us
  matrix products  533 us (55%)
  local copies, waits for them, and re-layouts  231 us (24%)
  waiting for transfers between devices  129 us (13%)
  other arithmetic  46.4 us (5%)
  starting transfers between devices  18.9 us (2%)
    dot_general x8, matrix products, edge_pass(): jnp.dot(hidden.reshape(-1, feat_width), edge_out, preferred_element_type=...  158 us
    dot_general x8, matrix products, edge_pass(): jnp.einsum('fbc,fcx->fbx', select_bf, dst_low, preferred_element_type=jnp...  151 us
    reshape x8, local copies, waits for them, and re-layouts, edge_pass(): near_dst = near_dst.reshape(own_src.shape)  141 us
    dot_general x8, matrix products, edge_pass(): jnp.einsum('fbc,fcx->fbx', select_bf, dst_high, preferred_element_type=jn...  57.1 us
    ppermute x2, waiting for transfers between devices, with_halo(): lax.ppermute(lax.slice_in_dim(block, block.shape[dim] - width, None, axis...  53.9 us
    all_to_all x1, waiting for transfers between devices, shards(): lax.all_to_all(mean_msg, 'tm', split_axis=1, concat_axis=0, tiled=True)  47.5 us
    convert_element_type x1, other arithmetic, split_parts(): low_part = (values - high_part.astype(jnp.float32)).astype(jnp.bfloat16)  29.6 us
    another operation x1, local copies, waits for them, and re-layouts, edge_pass(): flat_dst = other_dst.reshape(frames, other_blocks, block_len * feat_width)  28.5 us
  transfers between devices with their start and end apart: 6, of which 4 were waited for; matrix products, arithmetic and copies ran while one was open for 6% of the time, Pallas kernels for 0%

commit v1 on v0

--- a/solution.py
+++ b/solution.py
@@ -141,7 +141,10 @@
     )
     mean_msg = (summed / slot_count).astype(jnp.bfloat16).reshape(frames, local_rows, feat_width)
     new_positions = positions + (moved / slot_count).reshape(frames, 3, local_rows)
-    regrouped = lax.all_to_all(mean_msg, "tm", split_axis=1, concat_axis=0, tiled=True)
+    size = lax.axis_size("tm")
+    tiles = jnp.stack(jnp.split(mean_msg, size, axis=1), axis=0)
+    tiles = lax.all_to_all(tiles, "tm", split_axis=0, concat_axis=0)
+    regrouped = jnp.concatenate(tiles, axis=0)
     conv_all = spectral_conv(regrouped, spectral, regrouped.shape[0])
     conv_own = lax.all_to_all(conv_all, "tm", split_axis=0, concat_axis=1, tiled=True)
     node_pre = (

time: 967 us -> 956 us (0.989)
  local copies, waits for them, and re-layouts: 231 us -> 213 us
    reshape x1 -> x0, local copies, waits for them, and re-layouts: 10.8 us -> none  [shards(): (summed / slot_count).astype(jnp.bfloat16)]
    unnamed x136 -> x134, local copies, waits for them, and re-layouts: 23.7 us -> 20.7 us
where the time goes in v1:
time: 956 us; the launch traced here: 948 us
  matrix products  535 us (56%)
  local copies, waits for them, and re-layouts  213 us (22%)
  waiting for transfers between devices  129 us (13%)
  other arithmetic  50.3 us (5%)
  starting transfers between devices  19.1 us (2%)
    dot_general x8, matrix products, edge_pass(): jnp.dot(hidden.reshape(-1, feat_width), edge_out, preferred_element_type=...  158 us
    dot_general x8, matrix products, edge_pass(): jnp.einsum('fbc,fcx->fbx', select_bf, dst_low, preferred_element_type=jnp...  151 us
    reshape x8, local copies, waits for them, and re-layouts, edge_pass(): near_dst = near_dst.reshape(own_src.shape)  141 us
    dot_general x8, matrix products, edge_pass(): jnp.einsum('fbc,fcx->fbx', select_bf, dst_high, preferred_element_type=jn...  57 us
    ppermute x2, waiting for transfers between devices, with_halo(): lax.ppermute(lax.slice_in_dim(block, block.shape[dim] - width, None, axis...  53.9 us
    all_to_all x1, waiting for transfers between devices, shards(): tiles = lax.all_to_all(tiles, 'tm', split_axis=0, concat_axis=0)  47.5 us
    convert_element_type x1, other arithmetic, split_parts(): low_part = (values - high_part.astype(jnp.float32)).astype(jnp.bfloat16)  29.6 us
    another operation x1, local copies, waits for them, and re-layouts, edge_pass(): flat_dst = other_dst.reshape(frames, other_blocks, block_len * feat_width)  28.5 us
  transfers between devices with their start and end apart: 6, of which 4 were waited for; matrix products, arithmetic and copies ran while one was open for 6% of the time, Pallas kernels for 0%

profile of v1, /device:TPU:1, one launch (start us, length us, event | category | flops | bytes accessed | tf_op | source)
XLA Modules:
  0.0 948.1 jit_solution(8848774892831387748)
XLA Ops:
  14.3 10.3 %fusion.99 = f32[64,448,128]{2,1,0:T(8,128)} fusion(bf16[64,448,128]{2,1,0:T(8,128)(2,1)} %param.11, bf16[256,128]{1,0:T(8,128)(2,1)S(1)} %copy-done.47), kind=kOutput, calls=%fused_computation.190 | convolution fusion | flops 939524096 | bytes 22052864 | tf_op jit(solution)/shard_map/dot_general | solution.py:131
  26.8 53.9 %collective-permute-done.2 = bf16[64,3,192]{0,2,1:T(8,128)(2,1)S(1)} collective-permute-done((bf16[64,3,192]{0,2,1:T(8,128)(2,1)}, bf16[64,3,192]{0,2,1:T(8,128)(2,1)S(1)}, u32[]{:S(2)}, u32[]{:S(2)}) %collective-permute-start.2) | collective-permute-done | bytes 73760 | tf_op jit(solution)/shard_map/ppermute | solution.py:17
  106.6 13.9 %fusion.3 = f32[64,832,128]{2,1,0:T(8,128)} fusion(bf16[64,192,128]{2,1,0:T(8,128)(2,1)} %collective-permute-done.1, bf16[64,448,128]{2,1,0:T(8,128)(2,1)} %param.11, bf16[64,192,128]{2,1,0:T(8,128)(2,1)} %collective-permute-done, bf16[256,128]{1,0:T(8,128)(2,1)S(1)} %copy-done.47), kind=kOutput, calls=%fused_computation.37 | convolution fusion | flops 1785724928 | bytes 40927232 | tf_op jit(solution)/shard_map/dot_general | solution.py:136
  120.5 28.5 %reshape_reshape.6 = f32[64,26,4096]{2,1,0:T(8,128)} reshape(f32[64,832,128]{2,1,0:T(8,128)} %fusion.3) | data formatting | bytes 54525952 | tf_op jit(solution)/shard_map/reshape;reshape | solution.py:34
  148.9 29.6 %subtract_convert_fusion = (bf16[64,26,4096]{2,1,0:T(8,128)(2,1)}, bf16[64,26,4096]{2,1,0:T(8,128)(2,1)S(1)}) fusion(f32[64,26,4096]{2,1,0:T(8,128)} %reshape_reshape.6), kind=kLoop, calls=%fused_computation.5 | loop fusion | flops 27262976 | bytes 54525952 | tf_op jit(solution)/shard_map/convert_element_type | solution.py:27
  178.5 7.1 fusion.52
  185.6 7.1 fusion.51
  192.7 7.1 fusion.50
  199.8 7.4 fusion.49
  207.1 7.2 fusion.48
  214.3 7.1 fusion.47
  221.4 7.1 fusion.46
  228.5 7.1 fusion.45
  235.6 18.9 %convolution_add_fusion.3 = f32[64,14,4096]{2,1,0:T(8,128)} fusion(f32[64,14,4096]{2,1,0:T(8,128)} %fusion.52, bf16[64,26,4096]{2,1,0:T(8,128)(2,1)} %get-tuple-element.14, s32[64,14]{1,0:T(8,128)S(1)} %copy.110), kind=kOutput, calls=%fused_computation.47 | convolution fusion | flops 194580736 | bytes 42995200 | tf_op jit(solution)/shard_map/fbc,fcx->fbx/dot_general | solution.py:45
  254.5 17.7 %reshape.366 = f32[64,14,32,128]{3,2,1,0:T(8,128)} reshape(f32[64,14,4096]{2,1,0:T(8,128)} %convolution_add_fusion.3) | data formatting | bytes 29360128 | tf_op jit(solution)/shard_map/reshape | solution.py:46
  272.2 18.9 %convolution_add_fusion.4 = f32[64,14,4096]{2,1,0:T(8,128)} fusion(f32[64,14,4096]{2,1,0:T(8,128)} %fusion.51, bf16[64,26,4096]{2,1,0:T(8,128)(2,1)} %get-tuple-element.14, s32[64,14]{1,0:T(8,128)S(1)} %copy.105), kind=kOutput, calls=%fused_computation.48 | convolution fusion | flops 194580736 | bytes 42995200 | tf_op jit(solution)/shard_map/fbc,fcx->fbx/dot_general | solution.py:45
  291.1 17.5 %reshape.365 = f32[64,14,32,128]{3,2,1,0:T(8,128)} reshape(f32[64,14,4096]{2,1,0:T(8,128)} %convolution_add_fusion.4) | data formatting | bytes 29360128 | tf_op jit(solution)/shard_map/reshape | solution.py:46
  308.5 18.9 %convolution_add_fusion.5 = f32[64,14,4096]{2,1,0:T(8,128)} fusion(f32[64,14,4096]{2,1,0:T(8,128)} %fusion.50, bf16[64,26,4096]{2,1,0:T(8,128)(2,1)} %get-tuple-element.14, s32[64,14]{1,0:T(8,128)S(1)} %copy.100), kind=kOutput, calls=%fused_computation.49 | convolution fusion | flops 194580736 | bytes 42995200 | tf_op jit(solution)/shard_map/fbc,fcx->fbx/dot_general | solution.py:45
  327.4 17.5 %reshape.364 = f32[64,14,32,128]{3,2,1,0:T(8,128)} reshape(f32[64,14,4096]{2,1,0:T(8,128)} %convolution_add_fusion.5) | data formatting | bytes 29360128 | tf_op jit(solution)/shard_map/reshape | solution.py:46
  344.9 19.0 %convolution_add_fusion.6 = f32[64,14,4096]{2,1,0:T(8,128)} fusion(f32[64,14,4096]{2,1,0:T(8,128)} %fusion.49, bf16[64,26,4096]{2,1,0:T(8,128)(2,1)} %get-tuple-element.14, s32[64,14]{1,0:T(8,128)S(1)} %copy-done.39), kind=kOutput, calls=%fused_computation.50 | convolution fusion | flops 194580736 | bytes 42995200 | tf_op jit(solution)/shard_map/fbc,fcx->fbx/dot_general | solution.py:45
  363.9 17.8 %reshape.363 = f32[64,14,32,128]{3,2,1,0:T(8,128)} reshape(f32[64,14,4096]{2,1,0:T(8,128)} %convolution_add_fusion.6) | data formatting | bytes 29360128 | tf_op jit(solution)/shard_map/reshape | solution.py:46
  381.7 19.0 %convolution_add_fusion.7 = f32[64,14,4096]{2,1,0:T(8,128)} fusion(f32[64,14,4096]{2,1,0:T(8,128)} %fusion.48, bf16[64,26,4096]{2,1,0:T(8,128)(2,1)} %get-tuple-element.14, s32[64,14]{1,0:T(8,128)S(1)} %copy-done.37), kind=kOutput, calls=%fused_computation.51 | convolution fusion | flops 194580736 | bytes 42995200 | tf_op jit(solution)/shard_map/fbc,fcx->fbx/dot_general | solution.py:45
  400.7 17.5 %reshape.362 = f32[64,14,32,128]{3,2,1,0:T(8,128)} reshape(f32[64,14,4096]{2,1,0:T(8,128)} %convolution_add_fusion.7) | data formatting | bytes 29360128 | tf_op jit(solution)/shard_map/reshape | solution.py:46
  418.2 18.9 %convolution_add_fusion.8 = f32[64,14,4096]{2,1,0:T(8,128)} fusion(f32[64,14,4096]{2,1,0:T(8,128)} %fusion.47, bf16[64,26,4096]{2,1,0:T(8,128)(2,1)} %get-tuple-element.14, s32[64,14]{1,0:T(8,128)S(1)} %copy-done.35), kind=kOutput, calls=%fused_computation.52 | convolution fusion | flops 194580736 | bytes 42995200 | tf_op jit(solution)/shard_map/fbc,fcx->fbx/dot_general | solution.py:45
  437.1 17.5 %reshape.361 = f32[64,14,32,128]{3,2,1,0:T(8,128)} reshape(f32[64,14,4096]{2,1,0:T(8,128)} %convolution_add_fusion.8) | data formatting | bytes 29360128 | tf_op jit(solution)/shard_map/reshape | solution.py:46
  454.6 18.9 %convolution_add_fusion.9 = f32[64,14,4096]{2,1,0:T(8,128)} fusion(f32[64,14,4096]{2,1,0:T(8,128)} %fusion.46, bf16[64,26,4096]{2,1,0:T(8,128)(2,1)} %get-tuple-element.14, s32[64,14]{1,0:T(8,128)S(1)} %copy-done.33), kind=kOutput, calls=%fused_computation.53 | convolution fusion | flops 194580736 | bytes 42995200 | tf_op jit(solution)/shard_map/fbc,fcx->fbx/dot_general | solution.py:45
  473.5 17.6 %reshape.360 = f32[64,14,32,128]{3,2,1,0:T(8,128)} reshape(f32[64,14,4096]{2,1,0:T(8,128)} %convolution_add_fusion.9) | data formatting | bytes 29360128 | tf_op jit(solution)/shard_map/reshape | solution.py:46
  491.1 18.9 %convolution_add_fusion.10 = f32[64,14,4096]{2,1,0:T(8,128)} fusion(f32[64,14,4096]{2,1,0:T(8,128)} %fusion.45, bf16[64,26,4096]{2,1,0:T(8,128)(2,1)} %get-tuple-element.14, s32[64,14]{1,0:T(8,128)S(1)} %copy-done.31), kind=kOutput, calls=%fused_computation.54 | convolution fusion | flops 194580736 | bytes 42995200 | tf_op jit(solution)/shard_map/fbc,fcx->fbx/dot_general | solution.py:45
  510.1 17.6 %reshape.359 = f32[64,14,32,128]{3,2,1,0:T(8,128)} reshape(f32[64,14,4096]{2,1,0:T(8,128)} %convolution_add_fusion.10) | data formatting | bytes 29360128 | tf_op jit(solution)/shard_map/reshape | solution.py:46
  527.8 20.7 %divide_multiply_fusion = f32[64,14,32,128]{3,2,1,0:T(8,128)} fusion(f32[128]{0:T(128)S(1)} %copy-done.52, f32[64,14,32,128]{3,2,1,0:T(8,128)} %bitcast.226, f32[64,14,32,128]{3,2,1,0:T(8,128)} %reshape.366, f32[64,14,32]{2,1,0:T(8,128)S(1)} %copy-done.15, f32[128]{0:T(128)S(1)} %copy-done.53, f32[128]{0:T(128)S(1)} %copy-done.51, ...), kind=kOutput, calls=%fused_computation.21 | convolution fusion | flops 990904320 | bytes 44189184 | tf_op jit(solution)/shard_map/dot_general | solution.py:55
  548.5 16.6 %divide_multiply_fusion.1 = f32[64,14,32,128]{3,2,1,0:T(8,128)} fusion(f32[128]{0:T(128)S(1)} %copy-done.52, f32[64,14,32,128]{3,2,1,0:T(8,128)S(1)} %bitcast.230, f32[64,14,32,128]{3,2,1,0:T(8,128)} %reshape.365, f32[64,14,32]{2,1,0:T(8,128)S(1)} %copy-done.17, f32[128]{0:T(128)S(1)} %copy-done.53, f32[128]{0:T(128)S(1)} %copy-done.51, ...), kind=kOutput, calls=%fused_computation.23 | convolution fusion | flops 990904320 | bytes 44189184 | tf_op jit(solution)/shard_map/dot_general | solution.py:55
  565.2 10.9 %divide_multiply_fusion.2 = f32[64,14,32,128]{3,2,1,0:T(8,128)} fusion(f32[128]{0:T(128)S(1)} %copy-done.52, f32[64,14,32,128]{3,2,1,0:T(8,128)S(1)} %bitcast.231, f32[64,14,32,128]{3,2,1,0:T(8,128)S(1)} %bitcast.242, f32[64,14,32]{2,1,0:T(8,128)S(1)} %copy-done.19, f32[128]{0:T(128)S(1)} %copy-done.53, f32[128]{0:T(128)S(1)} %copy-done.51, ...), kind=kOutput, calls=%fused_computation.25 | convolution fusion | flops 990904320 | bytes 44189184 | tf_op jit(solution)/shard_map/dot_general | solution.py:55
  576.1 17.8 %divide_multiply_fusion.3 = f32[64,14,32,128]{3,2,1,0:T(8,128)} fusion(f32[128]{0:T(128)S(1)} %copy-done.52, f32[64,14,32,128]{3,2,1,0:T(8,128)S(1)} %bitcast.232, f32[64,14,32,128]{3,2,1,0:T(8,128)} %reshape.363, f32[64,14,32]{2,1,0:T(8,128)S(1)} %copy-done.21, f32[128]{0:T(128)S(1)} %copy-done.53, f32[128]{0:T(128)S(1)} %copy-done.51, ...), kind=kOutput, calls=%fused_computation.27 | convolution fusion | flops 990904320 | bytes 44189184 | tf_op jit(solution)/shard_map/dot_general | solution.py:55
  594.0 10.9 %divide_multiply_fusion.4 = f32[64,14,32,128]{3,2,1,0:T(8,128)} fusion(f32[128]{0:T(128)S(1)} %copy-done.52, f32[64,14,32,128]{3,2,1,0:T(8,128)S(1)} %bitcast.233, f32[64,14,32,128]{3,2,1,0:T(8,128)S(1)} %copy-done.3, f32[64,14,32]{2,1,0:T(8,128)S(1)} %copy-done.23, f32[128]{0:T(128)S(1)} %copy-done.53, f32[128]{0:T(128)S(1)} %copy-done.51, ...), kind=kOutput, calls=%fused_computation.29 | convolution fusion | flops 990904320 | bytes 44189184 | tf_op jit(solution)/shard_map/dot_general | solution.py:55
  604.8 17.8 %divide_multiply_fusion.5 = f32[64,14,32,128]{3,2,1,0:T(8,128)} fusion(f32[128]{0:T(128)S(1)} %copy-done.52, f32[64,14,32,128]{3,2,1,0:T(8,128)S(1)} %bitcast.234, f32[64,14,32,128]{3,2,1,0:T(8,128)} %reshape.361, f32[64,14,32]{2,1,0:T(8,128)S(1)} %copy-done.25, f32[128]{0:T(128)S(1)} %copy-done.53, f32[128]{0:T(128)S(1)} %copy-done.51, ...), kind=kOutput, calls=%fused_computation.31 | convolution fusion | flops 990904320 | bytes 44189184 | tf_op jit(solution)/shard_map/dot_general | solution.py:55
  622.7 10.9 %divide_multiply_fusion.6 = f32[64,14,32,128]{3,2,1,0:T(8,128)} fusion(f32[128]{0:T(128)S(1)} %copy-done.52, f32[64,14,32,128]{3,2,1,0:T(8,128)S(1)} %bitcast.235, f32[64,14,32,128]{3,2,1,0:T(8,128)S(1)} %copy-done.4, f32[64,14,32]{2,1,0:T(8,128)S(1)} %copy-done.27, f32[128]{0:T(128)S(1)} %copy-done.53, f32[128]{0:T(128)S(1)} %copy-done.51, ...), kind=kOutput, calls=%fused_computation.33 | convolution fusion | flops 990904320 | bytes 44189184 | tf_op jit(solution)/shard_map/dot_general | solution.py:55
  633.6 52.5 %multiply_reduce_fusion.7 = (f32[64,14,32]{2,1,0:T(8,128)}, f32[64,14,32]{2,1,0:T(8,128)}, f32[64,14,32]{2,1,0:T(8,128)}, f32[64,14,32]{2,1,0:T(8,128)}, f32[64,...) fusion(f32[128]{0:T(128)S(1)} %copy-done.55, ...), kind=kOutput, calls=%fused_computation.17 | convolution fusion | flops 1082425344 | bytes 140527616 | tf_op jit(solution)/shard_map/dot_general | solution.py:55
  700.7 47.5 %all-to-all-done = bf16[2,64,224,128]{3,2,1,0:T(8,128)(2,1)} async-done(((bf16[2,64,224,128]{3,2,1,0:T(8,128)(2,1)}), bf16[2,64,224,128]{3,2,1,0:T(8,128)(2,1)}, u32[]{:S(2)}, u32[]{:S(2)}) %all-to-all-start) | async-done | bytes 7340064 | tf_op jit(solution)/shard_map/all_to_all | solution.py:146
  748.2 11.2 %fusion.11 = f32[128,28672]{1,0:T(8,128)} fusion(bf16[16,8,224,128]{3,2,1,0:T(8,128)(2,1)} %bitcast.67, f32[64,128]{1,0:T(8,128)S(1)} %get-tuple-element.64, f32[64,128]{1,0:T(8,128)S(1)} %get-tuple-element.65), kind=kOutput, calls=%fused_computation.44 | convolution fusion | flops 939589632 | bytes 22085632 | tf_op jit(solution)/shard_map/dot_general | solution.py:77
  759.4 13.6 %fusion = bf16[128,28672]{1,0:T(8,128)(2,1)} fusion(f32[128,28672]{1,0:T(8,128)} %fusion.11, bf16[16,8,224,128]{3,2,1,0:T(8,128)(2,1)} %bitcast.67, f32[64,128]{1,0:T(8,128)S(1)} %get-tuple-element.64, f32[64,128]{1,0:T(8,128)S(1)} %get-tuple-element.65), kind=kOutput, calls=%fused_computation.3 | convolution fusion | flops 946946048 | bytes 29425664 | tf_op jit(solution)/shard_map/dot_general | solution.py:77
  800.6 14.5 %fusion.15 = f32[128,28672]{1,0:T(8,128)} fusion(f32[16,8,224,128]{3,2,1,0:T(8,128)S(1)} %bitcast.223, f32[128,64]{0,1:T(8,128)S(1)} %get-tuple-element.39, f32[128,64]{0,1:T(8,128)S(1)} %get-tuple-element.38), kind=kOutput, calls=%fused_computation.57 | convolution fusion | flops 939589632 | bytes 29425664 | tf_op jit(solution)/shard_map/dot_general | solution.py:99
  815.1 24.5 %convolution_add_fusion.1 = f32[128,28672]{1,0:T(8,128)} fusion(f32[128,28672]{1,0:T(8,128)} %fusion.15, f32[16,8,224,128]{3,2,1,0:T(8,128)} %bitcast.224, f32[128,64]{0,1:T(8,128)S(1)} %get-tuple-element.39, f32[128,64]{0,1:T(8,128)S(1)} %get-tuple-element.38), kind=kOutput, calls=%fused_computation.1 | convolution fusion | flops 943276032 | bytes 44105728 | tf_op jit(solution)/shard_map/dot_general | solution.py:100
  839.6 22.9 %fusion.16 = bf16[16,8,224,128]{3,1,2,0:T(8,128)(2,1)} fusion(f32[128,28672]{1,0:T(8,128)} %convolution_add_fusion.1, f32[16,8,224,128]{3,2,1,0:T(8,128)} %bitcast.225, f32[128,64]{0,1:T(8,128)S(1)} %get-tuple-element.39, f32[128,64]{0,1:T(8,128)S(1)} %get-tuple-element.38), kind=kOutput, calls=%fused_computation.58 | convolution fusion | flops 961609728 | bytes 36765696 | tf_op jit(solution)/shard_map/dot_general | solution.py:101
  862.5 7.8 copy.140
  877.2 12.7 %fusion.101 = f32[64,448,128]{2,1,0:T(8,128)} fusion(bf16[64,448,128]{2,1,0:T(8,128)(2,1)} %param.11, bf16[256,128]{1,0:T(8,128)(2,1)S(1)} %copy-done.48), kind=kOutput, calls=%fused_computation.192 | convolution fusion | flops 939524096 | bytes 22052864 | tf_op jit(solution)/shard_map/dot_general | solution.py:151
  900.6 25.3 %all-to-all-done.1 = bf16[128,224,128]{2,1,0:T(8,128)(2,1)} async-done(((bf16[128,224,128]{2,1,0:T(8,128)(2,1)}), bf16[128,224,128]{2,1,0:T(8,128)(2,1)}, u32[]{:S(2)}, u32[]{:S(2)}) %all-to-all-start.1) | async-done | bytes 7340064 | tf_op jit(solution)/shard_map/all_to_all | solution.py:149
  925.9 7.2 copy.115
  933.1 14.8 %add_convert_fusion = bf16[64,448,128]{2,1,0:T(8,128)(2,1)} fusion(bf16[64,448,128]{2,1,0:T(8,128)(2,1)} %param.11, f32[128]{0:T(128)S(1)} %get-tuple-element.37, f32[64,448,128]{2,1,0:T(8,128)} %fusion.101, bf16[64,448,128]{2,1,0:T(8,128)(2,1)} %bitcast.245, f32[128]{0:T(128)S(1)} %get-tuple-element.36, bf16[128,128]{1,0:T(8,128)(2,1)S(1)} %copy-done.54, ...), kind=kOutput, calls=%fused_computation.18 | convolution fusion | flops 1919418368 | bytes 36766720 | tf_op jit(solution)/shard_map/dot_general | solution.py:158
  (187 shorter events, 101.2 us)
Async XLA Ops:
  0.6 527.0 %copy-start = (bf16[128,128]{1,0:T(8,128)(2,1)S(1)}, bf16[128,128]{1,0:T(8,128)(2,1)}, u32[]{:S(2)}) copy-start(bf16[128,128]{1,0:T(8,128)(2,1)} %param.15) | copy-start | bytes 98308
  6.7 99.9 %collective-permute-start = (bf16[64,192,128]{2,1,0:T(8,128)(2,1)}, bf16[64,192,128]{2,1,0:T(8,128)(2,1)}, u32[]{:S(2)}, u32[]{:S(2)}) collective-permute-start(bf16[64,192,128]{2,1,0:T(8,128)(2,1)} %get-tuple-element.21), channel_id=1, source_target_pairs={{0,2},{2,4},{4,6},{6,8},{8,10},{10,12},{12,14},{14,16},{16,18},{18... | collective-permute-start | bytes 9437192 | tf_op jit(solution)/shard_map/ppermute | solution.py:17
  9.3 97.3 %collective-permute-start.1 = (bf16[64,192,128]{2,1,0:T(8,128)(2,1)}, bf16[64,192,128]{2,1,0:T(8,128)(2,1)}, u32[]{:S(2)}, u32[]{:S(2)}) collective-permute-start(bf16[64,192,128]{2,1,0:T(8,128)(2,1)} %get-tuple-element.22), channel_id=1, source_target_pairs={{2,0},{4,2},{6,4},{8,6},{10,8},{12,10},{14,12},{16,14},{18,16},{20... | collective-permute-start | bytes 9437192 | tf_op jit(solution)/shard_map/ppermute | solution.py:20
  11.4 69.3 %collective-permute-start.2 = (bf16[64,3,192]{0,2,1:T(8,128)(2,1)}, bf16[64,3,192]{0,2,1:T(8,128)(2,1)S(1)}, u32[]{:S(2)}, u32[]{:S(2)}) collective-permute-start(bf16[64,3,192]{0,2,1:T(8,128)(2,1)} %get-tuple-element.23), channel_id=1, source_target_pairs={{0,2},{2,4},{4,6},{6,8},{8,10},{10,12},{12,14},{14,16},{16,18},{18... | collective-permute-start | bytes 221192 | tf_op jit(solution)/shard_map/ppermute | solution.py:17
  13.2 69.9 %collective-permute-start.3 = (bf16[64,3,192]{0,2,1:T(8,128)(2,1)S(1)}, bf16[64,3,192]{0,2,1:T(8,128)(2,1)S(1)}, u32[]{:S(2)}, u32[]{:S(2)}) collective-permute-start(bf16[64,3,192]{0,2,1:T(8,128)(2,1)S(1)} %get-tuple-element.24), channel_id=1, source_target_pairs={{2,0},{4,2},{6,4},{8,6},{10,8},{12,10},{14,12},{16,14},{18,16},{20... | collective-permute-start | bytes 221192 | tf_op jit(solution)/shard_map/ppermute | solution.py:20
  26.4 173.4 %copy-start.38 = (s32[64,14]{1,0:T(8,128)}, s32[64,14]{1,0:T(8,128)S(1)}, u32[]{:S(2)}) copy-start(s32[64,14]{1,0:T(8,128)S(1)} %copy.95) | copy-start | bytes 10756
  26.5 180.6 %copy-start.36 = (s32[64,14]{1,0:T(8,128)}, s32[64,14]{1,0:T(8,128)S(1)}, u32[]{:S(2)}) copy-start(s32[64,14]{1,0:T(8,128)S(1)} %copy.90) | copy-start | bytes 10756
  26.6 187.7 %copy-start.34 = (s32[64,14]{1,0:T(8,128)}, s32[64,14]{1,0:T(8,128)S(1)}, u32[]{:S(2)}) copy-start(s32[64,14]{1,0:T(8,128)S(1)} %copy.85) | copy-start | bytes 10756
  26.7 194.7 %copy-start.32 = (s32[64,14]{1,0:T(8,128)}, s32[64,14]{1,0:T(8,128)S(1)}, u32[]{:S(2)}) copy-start(s32[64,14]{1,0:T(8,128)S(1)} %copy.80) | copy-start | bytes 10756
  26.8 201.7 %copy-start.30 = (s32[64,14]{1,0:T(8,128)}, s32[64,14]{1,0:T(8,128)S(1)}, u32[]{:S(2)}) copy-start(s32[64,14]{1,0:T(8,128)S(1)} %copy.73) | copy-start | bytes 10756
  327.4 17.5 %copy-start.39 = (s32[64,14]{1,0:T(8,128)S(1)}, s32[64,14]{1,0:T(8,128)}, u32[]{:S(2)}) copy-start(s32[64,14]{1,0:T(8,128)} %copy-done.38) | copy-start | bytes 10756
  363.9 17.9 %copy-start.37 = (s32[64,14]{1,0:T(8,128)S(1)}, s32[64,14]{1,0:T(8,128)}, u32[]{:S(2)}) copy-start(s32[64,14]{1,0:T(8,128)} %copy-done.36) | copy-start | bytes 10756
  400.7 17.5 %copy-start.35 = (s32[64,14]{1,0:T(8,128)S(1)}, s32[64,14]{1,0:T(8,128)}, u32[]{:S(2)}) copy-start(s32[64,14]{1,0:T(8,128)} %copy-done.34) | copy-start | bytes 10756
  437.1 17.5 %copy-start.33 = (s32[64,14]{1,0:T(8,128)S(1)}, s32[64,14]{1,0:T(8,128)}, u32[]{:S(2)}) copy-start(s32[64,14]{1,0:T(8,128)} %copy-done.32) | copy-start | bytes 10756
  473.5 17.6 %copy-start.31 = (s32[64,14]{1,0:T(8,128)S(1)}, s32[64,14]{1,0:T(8,128)}, u32[]{:S(2)}) copy-start(s32[64,14]{1,0:T(8,128)} %copy-done.30) | copy-start | bytes 10756
  510.0 17.7 %copy-start.15 = (f32[64,14,32]{2,1,0:T(8,128)S(1)}, f32[64,14,32]{2,1,0:T(8,128)}, u32[]{:S(2)}) copy-start(f32[64,14,32]{2,1,0:T(8,128)} %get-tuple-element.54) | copy-start | bytes 344068
  510.0 17.7 %copy-start.51 = (f32[128]{0:T(128)S(1)}, f32[128]{0:T(128)}, u32[]{:S(2)}) copy-start(f32[128]{0:T(128)} %get-tuple-element.33) | copy-start | bytes 1540
  510.0 17.7 %copy-start.52 = (f32[128]{0:T(128)S(1)}, f32[128]{0:T(128)}, u32[]{:S(2)}) copy-start(f32[128]{0:T(128)} %get-tuple-element.34) | copy-start | bytes 1540
  510.0 17.7 %copy-start.53 = (f32[128]{0:T(128)S(1)}, f32[128]{0:T(128)}, u32[]{:S(2)}) copy-start(f32[128]{0:T(128)} %get-tuple-element.35) | copy-start | bytes 1540
  510.0 38.4 %slice-start = ((s8[14680064]{0:T(1024)(128)(4,1)}), s8[2097152]{0:T(1024)(128)(4,1)S(1)}, s32[]{:S(2)}) async-start(s8[14680064]{0:T(1024)(128)(4,1)} %bitcast.228), calls=%async_computation.2 | async-start | bytes 4194304
  527.7 20.8 %slice-start.1 = ((s8[14680064]{0:T(1024)(128)(4,1)}), s8[4194304]{0:T(1024)(128)(4,1)S(1)}, s32[]{:S(2)}) async-start(s8[14680064]{0:T(1024)(128)(4,1)} %bitcast.228), calls=%async_computation.3 | async-start | bytes 8388608
  527.7 20.8 %slice-start.2 = ((s8[14680064]{0:T(1024)(128)(4,1)}), s8[4194304]{0:T(1024)(128)(4,1)S(1)}, s32[]{:S(2)}) async-start(s8[14680064]{0:T(1024)(128)(4,1)} %bitcast.228), calls=%async_computation.4 | async-start | bytes 8388608
  527.7 20.8 %slice-start.3 = ((s8[14680064]{0:T(1024)(128)(4,1)}), s8[4194304]{0:T(1024)(128)(4,1)S(1)}, s32[]{:S(2)}) async-start(s8[14680064]{0:T(1024)(128)(4,1)} %bitcast.228), calls=%async_computation.5 | async-start | bytes 8388608
  527.7 20.8 %copy-start.17 = (f32[64,14,32]{2,1,0:T(8,128)S(1)}, f32[64,14,32]{2,1,0:T(8,128)}, u32[]{:S(2)}) copy-start(f32[64,14,32]{2,1,0:T(8,128)} %get-tuple-element.52) | copy-start | bytes 344068
  527.7 37.4 %slice-start.4 = ((s8[14680064]{0:T(1024)(128)(4,1)}), s8[4194304]{0:T(1024)(128)(4,1)S(1)}, s32[]{:S(2)}) async-start(s8[14680064]{0:T(1024)(128)(4,1)} %bitcast.241), calls=%async_computation.6 | async-start | bytes 8388608
  527.8 37.4 %slice-start.5 = ((s8[14680064]{0:T(1024)(128)(4,1)}), s8[4194304]{0:T(1024)(128)(4,1)S(1)}, s32[]{:S(2)}) async-start(s8[14680064]{0:T(1024)(128)(4,1)} %bitcast.241), calls=%async_computation.7 | async-start | bytes 8388608
  548.5 16.7 %slice-start.6 = ((s8[14680064]{0:T(1024)(128)(4,1)}), s8[4194304]{0:T(1024)(128)(4,1)S(1)}, s32[]{:S(2)}) async-start(s8[14680064]{0:T(1024)(128)(4,1)} %bitcast.241), calls=%async_computation.8 | async-start | bytes 8388608
  548.5 16.7 %slice-start.7 = ((s8[14680064]{0:T(1024)(128)(4,1)}), s8[2097152]{0:T(1024)(128)(4,1)S(1)}, s32[]{:S(2)}) async-start(s8[14680064]{0:T(1024)(128)(4,1)} %bitcast.241), calls=%async_computation.9 | async-start | bytes 4194304
  548.5 16.7 %copy-start.19 = (f32[64,14,32]{2,1,0:T(8,128)S(1)}, f32[64,14,32]{2,1,0:T(8,128)}, u32[]{:S(2)}) copy-start(f32[64,14,32]{2,1,0:T(8,128)} %get-tuple-element.50) | copy-start | bytes 344068
  576.1 17.9 %copy-start.3 = (f32[64,14,32,128]{3,2,1,0:T(8,128)S(1)}, f32[64,14,32,128]{3,2,1,0:T(8,128)}, u32[]{:S(2)}) copy-start(f32[64,14,32,128]{3,2,1,0:T(8,128)} %reshape.362) | copy-start | bytes 44040196
  576.1 17.9 %copy-start.23 = (f32[64,14,32]{2,1,0:T(8,128)S(1)}, f32[64,14,32]{2,1,0:T(8,128)}, u32[]{:S(2)}) copy-start(f32[64,14,32]{2,1,0:T(8,128)} %get-tuple-element.46) | copy-start | bytes 344068
  604.8 17.9 %copy-start.4 = (f32[64,14,32,128]{3,2,1,0:T(8,128)S(1)}, f32[64,14,32,128]{3,2,1,0:T(8,128)}, u32[]{:S(2)}) copy-start(f32[64,14,32,128]{3,2,1,0:T(8,128)} %reshape.360) | copy-start | bytes 44040196
  604.8 17.9 %copy-start.27 = (f32[64,14,32]{2,1,0:T(8,128)S(1)}, f32[64,14,32]{2,1,0:T(8,128)}, u32[]{:S(2)}) copy-start(f32[64,14,32]{2,1,0:T(8,128)} %get-tuple-element.42) | copy-start | bytes 344068
  693.4 54.8 %all-to-all-start = ((bf16[2,64,224,128]{3,2,1,0:T(8,128)(2,1)}), bf16[2,64,224,128]{3,2,1,0:T(8,128)(2,1)}, u32[]{:S(2)}, u32[]{:S(2)}) async-start(bf16[2,64,224,128]{3,2,1,0:T(8,128)(2,1)} %pad_maximum_fusion.1), calls=%async_computation | async-start | bytes 14680064 | tf_op jit(solution)/shard_map/all_to_all | solution.py:146
  870.3 55.6 %all-to-all-start.1 = ((bf16[128,224,128]{2,1,0:T(8,128)(2,1)}), bf16[128,224,128]{2,1,0:T(8,128)(2,1)}, u32[]{:S(2)}, u32[]{:S(2)}) async-start(bf16[128,224,128]{2,1,0:T(8,128)(2,1)} %bitcast.240), calls=%async_computation.1 | async-start | bytes 14680064 | tf_op jit(solution)/shard_map/all_to_all | solution.py:149
  877.0 15.5 %copy-start.20 = (f32[64,14,32]{2,1,0:T(8,128)S(1)}, f32[64,14,32]{2,1,0:T(8,128)}, u32[]{:S(2)}) copy-start(f32[64,14,32]{2,1,0:T(8,128)} %get-tuple-element.50) | copy-start | bytes 344068
  877.1 15.5 %copy-start.22 = (f32[64,14,32]{2,1,0:T(8,128)S(1)}, f32[64,14,32]{2,1,0:T(8,128)}, u32[]{:S(2)}) copy-start(f32[64,14,32]{2,1,0:T(8,128)} %get-tuple-element.48) | copy-start | bytes 344068
  877.1 16.8 %copy-start.16 = (f32[64,14,32]{2,1,0:T(8,128)S(1)}, f32[64,14,32]{2,1,0:T(8,128)}, u32[]{:S(2)}) copy-start(f32[64,14,32]{2,1,0:T(8,128)} %get-tuple-element.54) | copy-start | bytes 344068
  877.1 16.8 %copy-start.18 = (f32[64,14,32]{2,1,0:T(8,128)S(1)}, f32[64,14,32]{2,1,0:T(8,128)}, u32[]{:S(2)}) copy-start(f32[64,14,32]{2,1,0:T(8,128)} %get-tuple-element.52) | copy-start | bytes 344068
  877.1 18.2 %copy-start.7 = (f32[64,3,14,32]{3,2,1,0:T(8,128)S(1)}, f32[64,3,14,32]{3,2,1,0:T(8,128)}, u32[]{:S(2)}) copy-start(f32[64,3,14,32]{3,2,1,0:T(8,128)} %get-tuple-element.55) | copy-start | bytes 1032196
  877.1 18.2 %copy-start.8 = (f32[64,3,14,32]{3,2,1,0:T(8,128)S(1)}, f32[64,3,14,32]{3,2,1,0:T(8,128)}, u32[]{:S(2)}) copy-start(f32[64,3,14,32]{3,2,1,0:T(8,128)} %get-tuple-element.53) | copy-start | bytes 1032196
  877.1 18.1 %copy-start.9 = (f32[64,3,14,32]{3,2,1,0:T(8,128)S(1)}, f32[64,3,14,32]{3,2,1,0:T(8,128)}, u32[]{:S(2)}) copy-start(f32[64,3,14,32]{3,2,1,0:T(8,128)} %get-tuple-element.51) | copy-start | bytes 1032196
  877.1 18.1 %copy-start.10 = (f32[64,3,14,32]{3,2,1,0:T(8,128)S(1)}, f32[64,3,14,32]{3,2,1,0:T(8,128)}, u32[]{:S(2)}) copy-start(f32[64,3,14,32]{3,2,1,0:T(8,128)} %get-tuple-element.49) | copy-start | bytes 1032196
  877.1 18.1 %copy-start.11 = (f32[64,3,14,32]{3,2,1,0:T(8,128)S(1)}, f32[64,3,14,32]{3,2,1,0:T(8,128)}, u32[]{:S(2)}) copy-start(f32[64,3,14,32]{3,2,1,0:T(8,128)} %get-tuple-element.47) | copy-start | bytes 1032196
  877.2 18.1 %copy-start.12 = (f32[64,3,14,32]{3,2,1,0:T(8,128)S(1)}, f32[64,3,14,32]{3,2,1,0:T(8,128)}, u32[]{:S(2)}) copy-start(f32[64,3,14,32]{3,2,1,0:T(8,128)} %get-tuple-element.45) | copy-start | bytes 1032196
  877.2 18.1 %copy-start.13 = (f32[64,3,14,32]{3,2,1,0:T(8,128)S(1)}, f32[64,3,14,32]{3,2,1,0:T(8,128)}, u32[]{:S(2)}) copy-start(f32[64,3,14,32]{3,2,1,0:T(8,128)} %get-tuple-element.43) | copy-start | bytes 1032196
  877.2 18.1 %copy-start.14 = (f32[64,3,14,32]{3,2,1,0:T(8,128)S(1)}, f32[64,3,14,32]{3,2,1,0:T(8,128)}, u32[]{:S(2)}) copy-start(f32[64,3,14,32]{3,2,1,0:T(8,128)} %get-tuple-element.41) | copy-start | bytes 1032196
  895.3 37.7 %copy-start.54 = (bf16[128,128]{1,0:T(8,128)(2,1)S(1)}, bf16[128,128]{1,0:T(8,128)(2,1)}, u32[]{:S(2)}) copy-start(bf16[128,128]{1,0:T(8,128)(2,1)} %param.20) | copy-start | bytes 98308
  (22 other events, 266.0 us)
